TPU v7x, 32 devices: a whole 2x2x4 slice. The times are simulated.
32 devices in a mesh: ka: 4 (over y, x), rp: 8 (over z, core).
Axes of the slice: x: 2, y: 2, z: 4, core: 2. Of those that a mesh axis runs over, the one named last changes fastest.
Arguments:
- coupling_table: bfloat16 [512, 256, 1024], P('ka', 'rp'), may hold values from -0.016479492 to 0.016479492
- k_points: int32 [3, 2048], P(None, 'ka'), may hold values from 0 to 15
- re_vectors: int32 [3, 512], replicated, may hold values from -6 to 6
- rp_vectors: int32 [3, 256], P(None, 'rp'), may hold values from -6 to 6
- q_points: int32 [3, 2], replicated, may hold values from 0 to 15
Outputs:
- bloch_coupling: float32 [2048, 2048], P(('ka', 'rp'))
All inputs are finite; a program needn't handle non-finite values.
Results may differ from a plain program's by a relative error of at most 0.0022.
Values may be sent and summed in bfloat16 or wider, within the bound.
A program may use at most 64 MiB of HBM per device.

v0:
```python
import math

import jax
import jax.numpy as jnp
from jax import lax
from jax.sharding import PartitionSpec as P

NKG = 16


def phases(left, right):
    nested = (
        left[0][:, None] * right[0][None, :]
        + left[1][:, None] * right[1][None, :]
        + left[2][:, None] * right[2][None, :]
    )
    wrapped = jnp.mod(nested, NKG)
    angles = wrapped.astype(jnp.float32) * (2.0 * math.pi / NKG)
    return (jnp.cos(angles), jnp.sin(angles))


def per_device(coupling_table, k_points, re_vectors, rp_vectors, q_points):
    high = lax.Precision.HIGHEST
    local_rp = coupling_table.shape[1]
    entries = coupling_table.shape[2] // 2
    waves = q_points.shape[1]
    q_cos, q_sin = phases(q_points, rp_vectors)
    k_cos, k_sin = phases(k_points, re_vectors)
    k_cos = k_cos.astype(jnp.bfloat16)
    k_sin = k_sin.astype(jnp.bfloat16)
    local_re = coupling_table.shape[0]
    values = coupling_table.astype(jnp.float32).reshape(local_re, local_rp, 2, entries)
    real_in = values[:, :, 0, :]
    imag_in = values[:, :, 1, :]
    real_mid = jnp.einsum("qr,erm->eqm", q_cos, real_in, precision=high) - jnp.einsum(
        "qr,erm->eqm", q_sin, imag_in, precision=high
    )
    imag_mid = jnp.einsum("qr,erm->eqm", q_sin, real_in, precision=high) + jnp.einsum(
        "qr,erm->eqm", q_cos, imag_in, precision=high
    )
    stacked = jnp.stack(
        [real_mid.reshape(local_re, waves * entries), imag_mid.reshape(local_re, waves * entries)],
        axis=0,
    )
    reduced = lax.psum_scatter(stacked, "rp", scatter_dimension=2, tiled=True)
    fragment = lax.all_gather(reduced, "ka", axis=1, tiled=True)
    cos_part = k_cos.astype(jnp.float32)
    sin_part = k_sin.astype(jnp.float32)
    real_add = jnp.dot(
        cos_part, fragment[0], precision=high, preferred_element_type=jnp.float32
    ) - jnp.dot(sin_part, fragment[1], precision=high, preferred_element_type=jnp.float32)
    imag_add = jnp.dot(
        sin_part, fragment[0], precision=high, preferred_element_type=jnp.float32
    ) + jnp.dot(cos_part, fragment[1], precision=high, preferred_element_type=jnp.float32)
    combined = jnp.stack([real_add, imag_add], axis=1)
    moved = lax.all_to_all(combined, "rp", split_axis=0, concat_axis=2, tiled=True)
    return moved.reshape(moved.shape[0], 2 * waves * entries)


def solution(mesh):
    placed = (P("ka", "rp", None), P(None, "ka"), P(), P(None, "rp"), P())
    return jax.shard_map(
        per_device, mesh=mesh, in_specs=placed, out_specs=P(("ka", "rp"), None), check_vma=False
    )
```

profile of v0, /device:TPU:1, one launch (start us, length us, event | category | flops | bytes accessed | tf_op | source)
XLA Modules:
  0.0 145.7 jit_solution(4808768817966968522)
XLA Ops:
  6.5 0.0 reduce-scatter.2.cloned.1.call-start
  6.5 0.8 slice_bitcast_fusion.8
  7.3 1.0 slice_reduce_fusion.2
  8.3 12.1 %copy.11 = bf16[128,32,1024]{0,2,1:T(8,128)(2,1)} copy(bf16[128,32,1024]{2,1,0:T(8,128)(2,1)} %param.5) | data formatting | bytes 16777216 | tf_op args[0]
  20.4 5.9 %fusion.52 = (bf16[128,32,1,512]{0,3,2,1:T(8,128)(2,1)}, bf16[128,32,1,512]{0,3,2,1:T(8,128)(2,1)}) fusion(bf16[128,32,2,512]{0,3,2,1:T(8,128)(2,1)} %bitcast.65), kind=kLoop, calls=%fused_computation.64 | loop fusion | bytes 16777216 | tf_op jit(solution)/shard_map/slice | solution.py:33
  26.3 8.0 %copy.17 = bf16[128,32,1,512]{3,1,0,2:T(8,128)(2,1)} copy(bf16[128,32,1,512]{0,3,2,1:T(8,128)(2,1)} %get-tuple-element.11) | data formatting | bytes 8388608
  34.3 0.1 fusion.50
  34.4 8.0 %copy.16 = bf16[128,32,1,512]{3,1,0,2:T(8,128)(2,1)} copy(bf16[128,32,1,512]{0,3,2,1:T(8,128)(2,1)} %get-tuple-element.10) | data formatting | bytes 8388608
  42.4 0.0 copy-start
  42.4 0.0 copy-start.1
  42.4 4.1 %fusion.2 = f32[2,128,512]{2,0,1:T(2,128)S(1)} fusion(bf16[128,32,1,512]{3,1,0,2:T(8,128)(2,1)} %copy.17, f32[2,32]{1,0:T(2,128)S(1)} %get-tuple-element.8), kind=kOutput, calls=%fused_computation.2 | convolution fusion | flops 50331648 | bytes 4718848 | tf_op jit(solution)/shard_map/qr,erm->eqm/dot_general | solution.py:35
  46.5 0.0 copy-done
  46.5 1.8 %fusion = f32[2,128,512]{2,0,1:T(2,128)S(1)} fusion(bf16[128,32,1,512]{3,1,0,2:T(8,128)(2,1)S(1)} %copy-done, f32[2,32]{1,0:T(2,128)S(1)} %cos.7), kind=kOutput, calls=%fused_computation | convolution fusion | flops 50331648 | bytes 4718848 | tf_op jit(solution)/shard_map/qr,erm->eqm/dot_general | solution.py:38
  48.3 0.0 copy-done.1
  48.3 1.8 %fusion.11 = f32[128,2,512]{2,1,0:T(2,128)S(1)} fusion(f32[2,128,512]{2,0,1:T(2,128)S(1)} %fusion.2, bf16[128,32,1,512]{3,1,0,2:T(8,128)(2,1)S(1)} %copy-done.1, f32[2,32]{1,0:T(2,128)S(1)} %cos.7), kind=kOutput, calls=%fused_computation.12 | convolution fusion | flops 50462720 | bytes 5243136 | tf_op jit(solution)/shard_map/qr,erm->eqm/dot_general | solution.py:35
  50.1 0.5 stack_reshape.6
  50.6 0.0 copy-start.2
  50.6 0.0 copy-start.3
  50.6 3.9 %fusion.17 = f32[128,2,512]{2,1,0:T(2,128)S(1)} fusion(f32[2,128,512]{2,0,1:T(2,128)S(1)} %fusion, bf16[128,32,1,512]{3,1,0,2:T(8,128)(2,1)} %copy.16, f32[2,32]{1,0:T(2,128)S(1)} %get-tuple-element.8), kind=kOutput, calls=%fused_computation.14 | convolution fusion | flops 50462720 | bytes 5243136 | tf_op jit(solution)/shard_map/qr,erm->eqm/dot_general | solution.py:38
  54.5 0.5 stack_reshape.7
  55.0 1.0 pad_maximum_fusion
  56.0 0.0 reduce-scatter.2.cloned.1.call-update
  56.1 0.0 copy-done.2
  56.1 0.0 copy-done.3
  56.1 31.2 %reduce-scatter.2.cloned.1.call-done = f32[2,128,128]{2,1,0:T(8,128)} async-done(((f32[2,128,1024]{2,1,0:T(8,128)}), f32[2,128,128]{2,1,0:T(8,128)}) %reduce-scatter.2.cloned.1.call-update) | async-done | bytes 131088 | tf_op jit(solution)/shard_map/reduce_scatter | solution.py:45
  87.3 9.3 %all_gather.3 = f32[2,512,128]{2,1,0:T(8,128)S(1)} all-gather(f32[2,128,128]{2,1,0:T(8,128)} %reduce-scatter.2.cloned.1.call-done), channel_id=1, replica_groups=mesh['ka'=4,'rp'=8] {'ka'}, dimensions={1}, use_global_device_ids=true | all-gather | bytes 655360 | tf_op jit(solution)/shard_map/all_gather | solution.py:46
  96.6 4.5 %fusion.25 = f32[512,128]{1,0:T(8,128)S(1)} fusion(s32[512]{0:T(512)S(1)} %bitcast.84, s32[512]{0:T(512)S(1)} %bitcast.72, s32[512]{0:T(512)S(1)} %bitcast.88, s32[512]{0:T(512)S(1)} %bitcast.76, s32[512]{0:T(512)S(1)} %bitcast.80, s32[512]{0:T(512)S(1)} %bitcast.68, f32[2,512,128]{2,1,0:T(8,128)S(1)} %all_gather.3), kind=kOutput, calls=%fused_computation.27 | convolution fusion | flops 407633920 | bytes 536576 | tf_op jit(solution)/shard_map/dot_general | solution.py:49
  101.1 4.6 %fusion.26 = f32[512,128]{1,0:T(8,128)S(1)} fusion(s32[512]{0:T(512)S(1)} %bitcast.85, s32[512]{0:T(512)S(1)} %bitcast.73, s32[512]{0:T(512)S(1)} %bitcast.89, s32[512]{0:T(512)S(1)} %bitcast.77, s32[512]{0:T(512)S(1)} %bitcast.81, s32[512]{0:T(512)S(1)} %bitcast.69, f32[2,512,128]{2,1,0:T(8,128)S(1)} %all_gather.3), kind=kOutput, calls=%fused_computation.28 | convolution fusion | flops 407633920 | bytes 536576 | tf_op jit(solution)/shard_map/dot_general | solution.py:52
  105.7 4.8 %fusion.21 = f32[512,1,128]{2,0,1:T(8,128)S(1)} fusion(f32[512,128]{1,0:T(8,128)S(1)} %fusion.25, s32[512]{0:T(512)S(1)} %bitcast.86, s32[512]{0:T(512)S(1)} %bitcast.74, s32[512]{0:T(512)S(1)} %bitcast.90, s32[512]{0:T(512)S(1)} %bitcast.78, s32[512]{0:T(512)S(1)} %bitcast.82, s32[512]{0:T(512)S(1)} %bitcast.70, f32[2,512,128]{2,1,0:T(8,128)S(1)} %all_gather.3), kind=kOutput, calls=%fused_computation.18 | convolution fusion | flops 407699456 | bytes 798720 | tf_op jit(solution)/shard_map/dot_general | solution.py:51
  110.5 4.5 %fusion.20 = f32[512,1,128]{2,0,1:T(8,128)S(1)} fusion(f32[512,128]{1,0:T(8,128)S(1)} %fusion.26, s32[512]{0:T(512)S(1)} %bitcast.87, s32[512]{0:T(512)S(1)} %bitcast.75, s32[512]{0:T(512)S(1)} %bitcast.91, s32[512]{0:T(512)S(1)} %bitcast.79, s32[512]{0:T(512)S(1)} %bitcast.83, s32[512]{0:T(512)S(1)} %bitcast.71, f32[2,512,128]{2,1,0:T(8,128)S(1)} %all_gather.3), kind=kOutput, calls=%fused_computation.16 | convolution fusion | flops 407699456 | bytes 798720 | tf_op jit(solution)/shard_map/dot_general | solution.py:54
  115.0 0.4 copy.14
  115.4 22.1 %all_to_all.15 = f32[512,2,128]{2,1,0:T(2,128)S(1)} all-to-all(f32[512,2,128]{2,1,0:T(2,128)S(1)} %copy.14), channel_id=1, replica_groups=mesh['ka'=4,'rp'=8] {'rp'}, dimensions={0} | all-to-all | bytes 1048576 | tf_op jit(solution)/shard_map/all_to_all | solution.py:56
  137.5 0.3 copy.15
  137.9 1.0 copy.20
  (4 shorter events, 0.1 us)
Async XLA Ops:
  6.5 80.8 %reduce-scatter.2.cloned.1.call-start = ((), (), s32[]{:S(2)}) async-start(), calls=%async_computation.2 | async-start | bytes 1179648 | tf_op jit(solution)/shard_map/reduce_scatter | solution.py:45
  42.4 4.1 %copy-start = (bf16[128,32,1,512]{3,1,0,2:T(8,128)(2,1)S(1)}, bf16[128,32,1,512]{3,1,0,2:T(8,128)(2,1)}, u32[]{:S(2)}) copy-start(bf16[128,32,1,512]{3,1,0,2:T(8,128)(2,1)} %copy.17) | copy-start | bytes 12582916
  42.4 5.9 %copy-start.1 = (bf16[128,32,1,512]{3,1,0,2:T(8,128)(2,1)S(1)}, bf16[128,32,1,512]{3,1,0,2:T(8,128)(2,1)}, u32[]{:S(2)}) copy-start(bf16[128,32,1,512]{3,1,0,2:T(8,128)(2,1)} %copy.16) | copy-start | bytes 12582916
  50.6 5.5 %copy-start.2 = (s32[3,512]{1,0:T(4,128)S(1)}, s32[3,512]{1,0:T(4,128)}, u32[]{:S(2)}) copy-start(s32[3,512]{1,0:T(4,128)} %param.6) | copy-start | bytes 18436
  50.6 5.5 %copy-start.3 = (s32[3,512]{1,0:T(4,128)S(1)}, s32[3,512]{1,0:T(4,128)}, u32[]{:S(2)}) copy-start(s32[3,512]{1,0:T(4,128)} %param.7) | copy-start | bytes 18436
Sparse Core Ops, SparseCore 0:
  56.2 31.0 reduce-scatter.1
where the time goes:
time: 148 us; the launch traced here: 146 us
  local copies, waits for them, and re-layouts  38.3 us (26%)
  blocking collectives  31.4 us (21%)
  waiting for transfers between devices  31.2 us (21%)
  matrix products  30 us (20%)
  between operations  13.5 us (9%)
    reduce_scatter x1, waiting for transfers between devices, per_device(): reduced = lax.psum_scatter(stacked, 'rp', scatter_dimension=2, tiled=True)  31.2 us
    unnamed x12, local copies, waits for them, and re-layouts  29 us
    all_to_all x1, blocking collectives, per_device(): lax.all_to_all(combined, 'rp', split_axis=0, concat_axis=2, tiled=True)  22.1 us
    all_gather x1, blocking collectives, per_device(): fragment = lax.all_gather(reduced, 'ka', axis=1, tiled=True)  9.28 us
    slice x1, local copies, waits for them, and re-layouts, per_device(): real_in = values[:, :, 0, :]  5.88 us
    dot_general x1, matrix products, per_device(): jnp.dot(sin_part, fragment[1], precision=high, preferred_element_type=jnp...  4.77 us
    dot_general x1, matrix products, per_device(): jnp.dot(sin_part, fragment[0], precision=high, preferred_element_type=jnp...  4.55 us
    dot_general x1, matrix products, per_device(): jnp.dot(cos_part, fragment[1], precision=high, preferred_element_type=jnp...  4.52 us
  transfers between devices with their start and end apart: 1, of which 1 were waited for; matrix products, arithmetic and copies ran while one was open for 0% of the time, Pallas kernels for 0%

commit v1 on v0

v1 whole, which is shorter than its diff:
```python
import functools
import math

import jax
import jax.numpy as jnp
import numpy as np
from jax import lax
from jax.experimental import pallas as pl
from jax.experimental.pallas import tpu as pltpu
from jax.sharding import PartitionSpec as P

NKG = 16
MESH = pl.DeviceIdType.MESH
GROUP = 8
CHUNK = 32

_B = np.arange(1.0, 5.0)
SINE = [
    float(c)
    for c in np.linalg.solve(
        _B[:, None] ** np.arange(1.0, 8.0, 2.0)[None, :], np.sin(_B * 2.0 * math.pi / NKG)
    )
]


def grid_sin(b):
    s = b * b
    return b * (SINE[0] + s * (SINE[1] + s * (SINE[2] + s * SINE[3])))


def grid_phases(n):
    n = n - NKG * jnp.floor(n * (1.0 / NKG))
    m = n - 4.0
    m = jnp.where(m < 0.0, m + NKG, m)
    return grid_sin(jnp.abs(n - 8.0) - 4.0), grid_sin(jnp.abs(m - 8.0) - 4.0)


def kernel(
    sizes, q_ref, k_ref, re_ref, rp_ref, table_ref, out_ref,
    table, lhs, partial, pair_in, z_out, z_in, frag, kn, kph, own, out_send, out_in,
    table_sem, pair_s, pair_r, z_s, z_r, ka_s, ka_r, o_s, o_r,
):
    n_ka, n_rp, E, R, M, Q, KL = sizes
    nz = n_rp // 2
    C = Q * M // n_rp
    Ec = min(CHUNK, E)
    NC = E // Ec
    ka = lax.axis_index("ka")
    me = lax.axis_index("rp")
    par = lax.rem(me, 2)
    zi = me // 2
    f32, bf16 = jnp.float32, jnp.bfloat16

    loads = []
    for c in range(NC):
        cp = pltpu.make_async_copy(
            table_ref.at[pl.ds(c * Ec * R, Ec * R)], table.at[pl.ds(c * Ec * R, Ec * R)],
            table_sem.at[c],
        )
        cp.start()
        loads.append(cp)

    barrier = pltpu.get_barrier_semaphore()
    for d in range(1, n_rp):
        pl.semaphore_signal(
            barrier, inc=1, device_id={"rp": lax.rem(me + d, n_rp)}, device_id_type=MESH
        )
    for d in range(1, n_ka):
        pl.semaphore_signal(
            barrier, inc=1, device_id={"ka": lax.rem(ka + d, n_ka)}, device_id_type=MESH
        )

    K = GROUP * R
    lane = lax.broadcasted_iota(jnp.int32, (GROUP, K), 1)
    row = lax.broadcasted_iota(jnp.int32, (GROUP, K), 0)
    keep = (lane >= row * R) & (lane < row * R + R)
    tiled = [jnp.concatenate([rp_ref[i : i + 1, :]] * GROUP, axis=1) for i in range(3)]
    parts = [[], []]
    for q in range(Q):
        n = q_ref[0, q] * tiled[0] + q_ref[1, q] * tiled[1] + q_ref[2, q] * tiled[2]
        for side, x in enumerate(grid_phases(n.astype(f32))):
            parts[side].append(jnp.where(keep, jnp.broadcast_to(x, (GROUP, K)), 0.0))
    exact = jnp.concatenate(parts[0] + parts[1], axis=0)
    high = exact.astype(bf16)
    half = 2 * Q * GROUP
    lhs[0:half, :] = high
    lhs[half : 2 * half, :] = (exact - high.astype(f32)).astype(bf16)

    def pair_copy(c):
        rows = pl.ds(c * Ec, Ec)
        return pltpu.make_async_remote_copy(
            src_ref=partial.at[1 - par, :, rows, :], dst_ref=pair_in.at[:, rows, :],
            send_sem=pair_s.at[c], recv_sem=pair_r.at[c],
            device_id={"rp": me + 1 - 2 * par}, device_id_type=MESH,
        )

    def z_copy(c, d):
        return pltpu.make_async_remote_copy(
            src_ref=z_out.at[c, d - 1], dst_ref=z_in.at[c, d - 1],
            send_sem=z_s.at[c, d - 1], recv_sem=z_r.at[c, d - 1],
            device_id={"rp": lax.rem(zi + d, nz) * 2 + par}, device_id_type=MESH,
        )

    def ka_copy(c, d):
        piece = frag.at[:, ka, pl.ds(c * Ec, Ec), :]
        return pltpu.make_async_remote_copy(
            src_ref=piece, dst_ref=piece,
            send_sem=ka_s.at[c, d - 1], recv_sem=ka_r.at[c, d - 1],
            device_id={"ka": lax.rem(ka + d, n_ka)}, device_id_type=MESH,
        )

    def out_copy(d):
        dest = lax.rem(me + d, n_rp)
        return pltpu.make_async_remote_copy(
            src_ref=out_send.at[d - 1], dst_ref=out_in.at[d - 1],
            send_sem=o_s.at[d - 1], recv_sem=o_r.at[d - 1],
            device_id={"rp": dest}, device_id_type=MESH,
        )

    def mid_sums(c):
        loads[c].wait()
        for g in range(Ec // GROUP):
            e0 = c * Ec + g * GROUP
            prod = jnp.dot(lhs[...], table[pl.ds(e0 * R, K), :], preferred_element_type=f32)
            prod = prod[:half] + prod[half:]
            cos_p, sin_p = prod[: half // 2], prod[half // 2 :]
            real = cos_p[:, :M] - sin_p[:, M:]
            imag = sin_p[:, :M] + cos_p[:, M:]
            for p in range(n_rp):
                q, col = (p * C) // M, (p * C) % M
                pick = slice(q * GROUP, (q + 1) * GROUP)
                block = jnp.concatenate(
                    [real[pick, col : col + C], imag[pick, col : col + C]], axis=1
                )
                partial[p % 2, p // 2, e0 : e0 + GROUP, :] = block

    def to_owners(c):
        pair_copy(c).wait()
        rows = pl.ds(c * Ec, Ec)
        for d in range(1, nz):
            j = lax.rem(zi + d, nz)
            z_out[c, d - 1] = (partial[par, j, rows, :] + pair_in[j, rows, :]).astype(bf16)
            z_copy(c, d).start()

    def to_groups(c):
        rows = pl.ds(c * Ec, Ec)
        total = partial[par, zi, rows, :] + pair_in[zi, rows, :]
        for d in range(1, nz):
            z_copy(c, d).wait()
            total = total + z_in[c, d - 1].astype(f32)
        high = total.astype(bf16)
        frag[0, ka, rows, :] = high
        frag[1, ka, rows, :] = (total - high.astype(f32)).astype(bf16)
        for d in range(1, n_ka):
            ka_copy(c, d).start()

    def k_block(p):
        cos_k, sin_k = grid_phases(kn[p * KL : (p + 1) * KL, :])
        kph[p, 0:KL, :] = cos_k.astype(bf16)
        kph[p, KL : 2 * KL, :] = sin_k.astype(bf16)

    ticks = NC + 2
    done = 0
    for t in range(ticks):
        if t < NC:
            mid_sums(t)
            if t == 0:
                pl.semaphore_wait(barrier, n_rp + n_ka - 2)
            pair_copy(t).start()
        if t == 0:
            kn[...] = lax.dot_general(
                k_ref[...].astype(f32).astype(bf16), re_ref[...].astype(f32).astype(bf16),
                (((0,), (0,)), ((), ())), preferred_element_type=f32,
            )
        upto = n_rp * (t + 1) // ticks
        for p in range(done, upto):
            k_block(p)
        done = upto
        if 1 <= t <= NC:
            to_owners(t - 1)
        if 2 <= t:
            to_groups(t - 2)

    for c in range(NC):
        for d in range(1, n_ka):
            src = frag.at[:, lax.rem(ka + n_ka - d, n_ka), pl.ds(c * Ec, Ec), :]
            ka_copy(c, d).wait_send()
            pltpu.make_async_remote_copy(
                src_ref=src, dst_ref=src,
                send_sem=ka_s.at[c, d - 1], recv_sem=ka_r.at[c, d - 1],
                device_id={"ka": lax.rem(ka + d, n_ka)}, device_id_type=MESH,
            ).wait_recv()

    def coupling(dest):
        ph = kph[dest]
        mid = frag[...].reshape(2, n_ka * E, 2 * C)
        s = jnp.dot(ph, mid[0], preferred_element_type=f32)
        s = s + jnp.dot(ph, mid[1], preferred_element_type=f32)
        real = s[:KL, :C] - s[KL:, C:]
        imag = s[KL:, :C] + s[:KL, C:]
        return jnp.concatenate([real, imag], axis=1)

    for d in range(1, n_rp):
        out_send[d - 1] = coupling(lax.rem(me + d, n_rp)).astype(bf16)
        out_copy(d).start()
    own[...] = coupling(me)

    for d in range(1, n_rp):
        out_copy(d).wait()
    for s in range(n_rp):
        lo, hi = s * C, Q * M + s * C

        @pl.when(me == s)
        def _():
            out_ref[:, lo : lo + C] = own[:, :C]
            out_ref[:, hi : hi + C] = own[:, C:]

        @pl.when(me != s)
        def _():
            block = out_in[lax.rem(me - s + n_rp, n_rp) - 1].astype(f32)
            out_ref[:, lo : lo + C] = block[:, :C]
            out_ref[:, hi : hi + C] = block[:, C:]


def per_device(mesh, coupling_table, k_points, re_vectors, rp_vectors, q_points):
    n_ka, n_rp = mesh.shape["ka"], mesh.shape["rp"]
    E, R, width = coupling_table.shape
    M, Q = width // 2, q_points.shape[1]
    kt = k_points.shape[1]
    KL = kt // n_rp
    nz, C = n_rp // 2, Q * M // n_rp
    Ec = min(CHUNK, E)
    NC = E // Ec
    f32, bf16 = jnp.float32, jnp.bfloat16
    dma = pltpu.SemaphoreType.DMA
    vmem = pl.BlockSpec(memory_space=pltpu.VMEM)
    return pl.pallas_call(
        functools.partial(kernel, (n_ka, n_rp, E, R, M, Q, KL)),
        out_shape=jax.ShapeDtypeStruct((KL, 2 * Q * M), f32),
        in_specs=[
            pl.BlockSpec(memory_space=pltpu.SMEM), vmem, vmem, vmem,
            pl.BlockSpec(memory_space=pl.ANY),
        ],
        out_specs=vmem,
        scratch_shapes=[
            pltpu.VMEM((E * R, width), bf16),
            pltpu.VMEM((4 * Q * GROUP, GROUP * R), bf16),
            pltpu.VMEM((2, nz, E, 2 * C), f32),
            pltpu.VMEM((nz, E, 2 * C), f32),
            pltpu.VMEM((NC, nz - 1, Ec, 2 * C), bf16),
            pltpu.VMEM((NC, nz - 1, Ec, 2 * C), bf16),
            pltpu.VMEM((2, n_ka, E, 2 * C), bf16),
            pltpu.VMEM((kt, n_ka * E), f32),
            pltpu.VMEM((n_rp, 2 * KL, n_ka * E), bf16),
            pltpu.VMEM((KL, 2 * C), f32),
            pltpu.VMEM((n_rp - 1, KL, 2 * C), bf16),
            pltpu.VMEM((n_rp - 1, KL, 2 * C), bf16),
            dma((NC,)), dma((NC,)), dma((NC,)), dma((NC, nz - 1)), dma((NC, nz - 1)),
            dma((NC, n_ka - 1)), dma((NC, n_ka - 1)), dma((n_rp - 1,)), dma((n_rp - 1,)),
        ],
        compiler_params=pltpu.CompilerParams(
            collective_id=0, has_side_effects=True, vmem_limit_bytes=40 * 1024 * 1024
        ),
        name="interpolate",
    )(q_points, k_points, re_vectors, rp_vectors, coupling_table.reshape(E * R, width))


def solution(mesh):
    placed = (P("ka", "rp", None), P(None, "ka"), P(), P(None, "rp"), P())
    return jax.shard_map(
        functools.partial(per_device, mesh), mesh=mesh, in_specs=placed,
        out_specs=P(("ka", "rp"), None), check_vma=False,
    )
```

time: 148 us -> 35.4 us (0.24); the launches traced: 146 us -> 35.1 us
  blocking collectives: 31.4 us -> 0 us
  local copies, waits for them, and re-layouts: 38.3 us -> 7.01 us
  waiting for transfers between devices: 31.2 us -> 0 us
  matrix products: 30 us -> 0 us
  Pallas kernels: 0 us -> 28.1 us
  between operations: 13.5 us -> 0.01 us
    reduce_scatter x1 -> x0, waiting for transfers between devices: 31.2 us -> none  [per_device(): reduced = lax.psum_scatter(stacked, 'rp', scatter_dimension=2, tiled=True)]
    dot_general x8 -> x0, matrix products: 30 us -> none  [the longest x1 4.77 us: per_device(): jnp.dot(sin_part, fragment[1], precision=high, preferred_element_type=jnp...]
    pallas_call x0 -> x1, Pallas kernels: none -> 28.1 us  [per_device(): pl.pallas_call(functools.partial(kernel, (n_ka, n_rp, E, R, M, Q, KL)), o...]
    all_to_all x1 -> x0, blocking collectives: 22.1 us -> none  [per_device(): lax.all_to_all(combined, 'rp', split_axis=0, concat_axis=2, tiled=True)]
    unnamed x12 -> x10, local copies, waits for them, and re-layouts: 29 us -> 7.01 us
    all_gather x1 -> x0, blocking collectives: 9.28 us -> none  [per_device(): fragment = lax.all_gather(reduced, 'ka', axis=1, tiled=True)]
    slice x4 -> x0, local copies, waits for them, and re-layouts: 6.9 us -> none  [the longest x1 5.88 us: per_device(): real_in = values[:, :, 0, :]]
  transfers between devices with their start and end apart: 1 -> 0, of which waited for: 1 -> 0; matrix products, arithmetic and copies ran while one was open for 0% -> 0% of each run, Pallas kernels for 0% -> 0%
where the time goes in v1:
time: 35.4 us; the launch traced here: 35.1 us
  Pallas kernels  28.1 us (79%)
  local copies, waits for them, and re-layouts  7.01 us (20%)
    pallas_call x1, Pallas kernels, per_device(): pl.pallas_call(functools.partial(kernel, (n_ka, n_rp, E, R, M, Q, KL)), o...  28.1 us
    unnamed x10, local copies, waits for them, and re-layouts  7.01 us

profile of v1, /device:TPU:1, one launch (start us, length us, event | category | flops | bytes accessed | tf_op | source)
XLA Modules:
  0.0 35.1 jit_solution(10077397918501509462)
XLA Ops:
  0.0 0.8 %copy.6.q_ref = s32[3,2]{1,0:T(4,128)S(1)} copy(s32[3,2]{0,1:T(2,128)} %param.9) | data formatting | bytes 48 | tf_op args[4]
  0.8 0.0 copy-start
  0.8 3.4 %copy-done = bf16[128,32,1024]{2,1,0:T(8,128)(2,1)S(1)} copy-done((bf16[128,32,1024]{2,1,0:T(8,128)(2,1)S(1)}, bf16[128,32,1024]{2,1,0:T(8,128)(2,1)}, u32[]{:S(2)}) %copy-start) | copy-done | bytes 8388632
  4.1 0.0 copy-start.1
  4.1 0.7 %copy-done.1 = s32[3,512]{1,0:T(4,128)S(1)} copy-done((s32[3,512]{1,0:T(4,128)S(1)}, s32[3,512]{1,0:T(4,128)}, u32[]{:S(2)}) %copy-start.1) | copy-done | bytes 6168
  4.8 0.0 copy-start.2
  4.8 0.7 %copy-done.2 = s32[3,512]{1,0:T(4,128)S(1)} copy-done((s32[3,512]{1,0:T(4,128)S(1)}, s32[3,512]{1,0:T(4,128)}, u32[]{:S(2)}) %copy-start.2) | copy-done | bytes 6168
  5.5 0.0 copy-start.3
  5.5 0.7 %copy-done.3 = s32[3,32]{1,0:T(4,128)S(1)} copy-done((s32[3,32]{1,0:T(4,128)S(1)}, s32[3,32]{1,0:T(4,128)}, u32[]{:S(2)}) %copy-start.3) | copy-done | bytes 408
  6.2 28.1 %interpolate.1 = f32[64,2048]{1,0:T(8,128)S(1)} custom-call(s32[3,2]{1,0:T(4,128)S(1)} %copy.6.q_ref, s32[3,512]{1,0:T(4,128)S(1)} %copy-done.1, s32[3,512]{1,0:T(4,128)S(1)} %copy-done.2, s32[3,32]{1,0:T(4,128)S(1)} %copy-done.3, bf16[4096,1024]{1,0:T(8,128)(2,1)S(1)} %bitcast.1), custom_call_target="tpu_custom_call" | custom-call | tf_op jit(solution)/shard_map/interpolate/pallas_call | solution.py:237
  34.4 0.8 %copy.8 = f32[64,2048]{1,0:T(8,128)} copy(f32[64,2048]{1,0:T(8,128)S(1)} %interpolate.1) | data formatting | bytes 1048576
Async XLA Ops:
  0.8 3.4 %copy-start = (bf16[128,32,1024]{2,1,0:T(8,128)(2,1)S(1)}, bf16[128,32,1024]{2,1,0:T(8,128)(2,1)}, u32[]{:S(2)}) copy-start(bf16[128,32,1024]{2,1,0:T(8,128)(2,1)} %param.5) | copy-start | bytes 25165828
  4.1 0.7 %copy-start.1 = (s32[3,512]{1,0:T(4,128)S(1)}, s32[3,512]{1,0:T(4,128)}, u32[]{:S(2)}) copy-start(s32[3,512]{1,0:T(4,128)} %k_ref.1) | copy-start | bytes 18436
  4.8 0.7 %copy-start.2 = (s32[3,512]{1,0:T(4,128)S(1)}, s32[3,512]{1,0:T(4,128)}, u32[]{:S(2)}) copy-start(s32[3,512]{1,0:T(4,128)} %re_ref.1) | copy-start | bytes 18436
  5.5 0.7 %copy-start.3 = (s32[3,32]{1,0:T(4,128)S(1)}, s32[3,32]{1,0:T(4,128)}, u32[]{:S(2)}) copy-start(s32[3,32]{1,0:T(4,128)} %rp_ref.1) | copy-start | bytes 1156

commit v2 on v1

--- a/solution.py
+++ b/solution.py
@@ -14,6 +14,8 @@
 GROUP = 8
 CHUNK = 32
 
+LAG = 1
+
 _B = np.arange(1.0, 5.0)
 SINE = [
     float(c)
@@ -36,9 +38,9 @@
 
 
 def kernel(
-    sizes, q_ref, k_ref, re_ref, rp_ref, table_ref, out_ref,
-    table, lhs, partial, pair_in, z_out, z_in, frag, kn, kph, own, out_send, out_in,
-    table_sem, pair_s, pair_r, z_s, z_r, ka_s, ka_r, o_s, o_r,
+    sizes, q_hbm, k_hbm, re_hbm, rp_hbm, table_ref, out_ref,
+    q_ref, k_ref, re_ref, rp_ref, table, lhs, partial, pair_in, z_out, z_in, frag, kn, kph, own, out_send, out_in,
+    small_sem, table_sem, pair_s, pair_r, z_s, z_r, ka_s, ka_r, o_s, o_r,
 ):
     n_ka, n_rp, E, R, M, Q, KL = sizes
     nz = n_rp // 2
@@ -51,6 +53,13 @@
     zi = me // 2
     f32, bf16 = jnp.float32, jnp.bfloat16
 
+    small = []
+    for i, (src, dst) in enumerate(
+        ((q_hbm, q_ref), (rp_hbm, rp_ref), (k_hbm, k_ref), (re_hbm, re_ref))
+    ):
+        cp = pltpu.make_async_copy(src, dst, small_sem.at[i])
+        cp.start()
+        small.append(cp)
     loads = []
     for c in range(NC):
         cp = pltpu.make_async_copy(
@@ -70,6 +79,8 @@
             barrier, inc=1, device_id={"ka": lax.rem(ka + d, n_ka)}, device_id_type=MESH
         )
 
+    small[0].wait()
+    small[1].wait()
     K = GROUP * R
     lane = lax.broadcasted_iota(jnp.int32, (GROUP, K), 1)
     row = lax.broadcasted_iota(jnp.int32, (GROUP, K), 0)
@@ -77,7 +88,7 @@
     tiled = [jnp.concatenate([rp_ref[i : i + 1, :]] * GROUP, axis=1) for i in range(3)]
     parts = [[], []]
     for q in range(Q):
-        n = q_ref[0, q] * tiled[0] + q_ref[1, q] * tiled[1] + q_ref[2, q] * tiled[2]
+        n = sum(q_ref[q : q + 1, i : i + 1] * tiled[i] for i in range(3))
         for side, x in enumerate(grid_phases(n.astype(f32))):
             parts[side].append(jnp.where(keep, jnp.broadcast_to(x, (GROUP, K)), 0.0))
     exact = jnp.concatenate(parts[0] + parts[1], axis=0)
@@ -159,27 +170,25 @@
         kph[p, 0:KL, :] = cos_k.astype(bf16)
         kph[p, KL : 2 * KL, :] = sin_k.astype(bf16)
 
-    ticks = NC + 2
-    done = 0
-    for t in range(ticks):
-        if t < NC:
-            mid_sums(t)
-            if t == 0:
-                pl.semaphore_wait(barrier, n_rp + n_ka - 2)
-            pair_copy(t).start()
-        if t == 0:
-            kn[...] = lax.dot_general(
-                k_ref[...].astype(f32).astype(bf16), re_ref[...].astype(f32).astype(bf16),
-                (((0,), (0,)), ((), ())), preferred_element_type=f32,
-            )
-        upto = n_rp * (t + 1) // ticks
-        for p in range(done, upto):
-            k_block(p)
-        done = upto
-        if 1 <= t <= NC:
-            to_owners(t - 1)
-        if 2 <= t:
-            to_groups(t - 2)
+    for c in range(NC):
+        mid_sums(c)
+        if c == 0:
+            pl.semaphore_wait(barrier, n_rp + n_ka - 2)
+        pair_copy(c).start()
+        if c >= LAG:
+            to_owners(c - LAG)
+    for c in range(max(NC - LAG, 0), NC):
+        to_owners(c)
+    small[2].wait()
+    small[3].wait()
+    kn[...] = lax.dot_general(
+        k_ref[...].astype(f32).astype(bf16), re_ref[...].astype(f32).astype(bf16),
+        (((0,), (0,)), ((), ())), preferred_element_type=f32,
+    )
+    for p in range(n_rp):
+        k_block(p)
+    for c in range(NC):
+        to_groups(c)
 
     for c in range(NC):
         for d in range(1, n_ka):
@@ -237,12 +246,13 @@
     return pl.pallas_call(
         functools.partial(kernel, (n_ka, n_rp, E, R, M, Q, KL)),
         out_shape=jax.ShapeDtypeStruct((KL, 2 * Q * M), f32),
-        in_specs=[
-            pl.BlockSpec(memory_space=pltpu.SMEM), vmem, vmem, vmem,
-            pl.BlockSpec(memory_space=pl.ANY),
-        ],
+        in_specs=[pl.BlockSpec(memory_space=pltpu.HBM)] * 5,
         out_specs=vmem,
         scratch_shapes=[
+            pltpu.VMEM((Q, 3), jnp.int32),
+            pltpu.VMEM(k_points.shape, jnp.int32),
+            pltpu.VMEM(re_vectors.shape, jnp.int32),
+            pltpu.VMEM(rp_vectors.shape, jnp.int32),
             pltpu.VMEM((E * R, width), bf16),
             pltpu.VMEM((4 * Q * GROUP, GROUP * R), bf16),
             pltpu.VMEM((2, nz, E, 2 * C), f32),
@@ -255,14 +265,14 @@
             pltpu.VMEM((KL, 2 * C), f32),
             pltpu.VMEM((n_rp - 1, KL, 2 * C), bf16),
             pltpu.VMEM((n_rp - 1, KL, 2 * C), bf16),
-            dma((NC,)), dma((NC,)), dma((NC,)), dma((NC, nz - 1)), dma((NC, nz - 1)),
+            dma((4,)), dma((NC,)), dma((NC,)), dma((NC,)), dma((NC, nz - 1)), dma((NC, nz - 1)),
             dma((NC, n_ka - 1)), dma((NC, n_ka - 1)), dma((n_rp - 1,)), dma((n_rp - 1,)),
         ],
         compiler_params=pltpu.CompilerParams(
-            collective_id=0, has_side_effects=True, vmem_limit_bytes=40 * 1024 * 1024
+            collective_id=0, has_side_effects=True, vmem_limit_bytes=67043328
         ),
         name="interpolate",
-    )(q_points, k_points, re_vectors, rp_vectors, coupling_table.reshape(E * R, width))
+    )(q_points.T, k_points, re_vectors, rp_vectors, coupling_table.reshape(E * R, width))
 
 
 def solution(mesh):

time: 35.4 us -> 28 us (0.79)
  local copies, waits for them, and re-layouts: 7.01 us -> 1.87 us
  Pallas kernels: 28.1 us -> 26 us
    unnamed x10 -> x1, local copies, waits for them, and re-layouts: 7.01 us -> 1.87 us
    pallas_call x1, Pallas kernels: 28.1 us -> 26 us  [per_device(): pl.pallas_call(functools.partial(kernel, (n_ka, n_rp, E, R, M, Q, KL)), o...]
where the time goes in v2:
time: 28 us; the launch traced here: 27.9 us
  Pallas kernels  26 us (93%)
  local copies, waits for them, and re-layouts  1.87 us (7%)
    pallas_call x1, Pallas kernels, per_device(): pl.pallas_call(functools.partial(kernel, (n_ka, n_rp, E, R, M, Q, KL)), o...  26 us
    unnamed x1, local copies, waits for them, and re-layouts  1.87 us

profile of v2, /device:TPU:1, one launch (start us, length us, event | category | flops | bytes accessed | tf_op | source)
XLA Modules:
  0.0 27.9 jit_solution(15238204341592162549)
XLA Ops:
  0.0 26.0 %interpolate.1 = f32[64,2048]{1,0:T(8,128)} custom-call(s32[2,3]{1,0:T(2,128)} %bitcast.3, s32[3,512]{1,0:T(4,128)} %k_hbm.1, s32[3,512]{1,0:T(4,128)} %re_hbm.1, s32[3,32]{1,0:T(4,128)} %rp_hbm.1, bf16[4096,1024]{1,0:T(8,128)(2,1)} %bitcast.2), custom_call_target="tpu_custom_call" | custom-call | tf_op jit(solution)/shard_map/interpolate/pallas_call | solution.py:246
  26.0 1.9 %copy.7 = f32[64,2048]{1,0:T(8,128)} copy(f32[64,2048]{1,0:T(8,128)} %interpolate.1) | data formatting | bytes 1048576
